TPU v7x, 256 devices: a whole 4x4x8 slice. The times are simulated.
256 devices in a mesh: cfg: 2 (over y_hi), seq: 128 (over y_lo, x, z, core).
Axes of the slice: x: 4, y: 4 (y_hi: 2, y_lo: 2; y = y_hi * 2 + y_lo), z: 8, core: 2. Of those that a mesh axis runs over, the one named last changes fastest.
Arguments:
- hidden: bfloat16 [2, 6144, 3072], P('cfg', 'seq'), may hold values from -3 to 3
- queries: bfloat16 [2, 6144, 2048], P('cfg', 'seq'), may hold values from -5 to 5
- key_proj: bfloat16 [2, 6144, 2048], P('cfg', 'seq'), may hold values from -5 to 5
- value_proj: bfloat16 [2, 6144, 2048], P('cfg', 'seq'), may hold values from -12 to 12
- norm_gain: float32 [2, 64], replicated, may hold values from 0.1 to 1.9
- norm_bias: float32 [2, 64], replicated, may hold values from -2 to 2
- positions: int32 [3, 6144], P(None, 'seq'), may hold values from 0 to 47
- text_len: int32 [2], P('cfg'), may hold values from 1 to 226
- time_embed: bfloat16 [512], replicated, may hold values from -6 to 6
- gate_table: bfloat16 [512, 3072], P(None, 'seq'), may hold values from -0.25 to 0.25
- mod_table: bfloat16 [512, 6144], P(None, 'seq'), may hold values from -0.25 to 0.25
- out_weight: bfloat16 [2048, 3072], P(None, ('cfg', 'seq')), may hold values from -0.125 to 0.125
- proj_weight: bfloat16 [3072, 64], replicated, may hold values from -0.109375 to 0.109375
- proj_bias: float32 [64], replicated, may hold values from -3 to 3
- latent: float32 [6144, 64], P('seq'), may hold values from -6 to 6
- solver_coef: float32 [2, 50], replicated, may hold values from 0.3 to 1.2
- step_index: int32 [1], replicated, may hold values from 0 to 49
Outputs:
- latent_next: float32 [6144, 64], P('seq', 'cfg')
All inputs are finite; a program needn't handle non-finite values.
Results may differ from a plain program's by a relative error of at most 0.0072.
Values may be sent and summed in bfloat16 or wider, within the bound.
No kernel may reach another device: no remote copies, remote signals or barrier semaphores. Data moves between devices by JAX's collectives and lax.ppermute only.
A program may use at most 128 MiB of HBM per device.

v0:
```python
import math
import jax
import jax.numpy as jnp
import numpy as np
from jax import lax
from jax.sharding import PartitionSpec as P

TEXT_SLOTS = 256
GUIDANCE = 6.0


def swapped(value, axis, bit):
    return lax.ppermute(value, axis, [(i, i ^ 1 << bit) for i in range(lax.axis_size(axis))])


def layer_norm(values, epsilon):
    centre = jnp.mean(values, axis=-1, keepdims=True)
    centred = values - centre
    variance = jnp.mean(centred * centred, axis=-1, keepdims=True)
    return centred * lax.rsqrt(variance + epsilon)


def rotary_angles(positions):
    pos_float = positions.astype(jnp.float32)
    time_freq = jnp.asarray(10000.0 ** (-2.0 * np.arange(8) / 16.0), jnp.float32)
    space_freq = jnp.asarray(10000.0 ** (-2.0 * np.arange(12) / 24.0), jnp.float32)
    return jnp.concatenate(
        [
            pos_float[0][:, None] * time_freq[None, :],
            pos_float[1][:, None] * space_freq[None, :],
            pos_float[2][:, None] * space_freq[None, :],
        ],
        axis=1,
    )


def norm_rotate(values, gain_row, offset, angles, is_video):
    row_count = values.shape[0]
    head_count = values.shape[1] // 64
    normed = (
        layer_norm(values.astype(jnp.float32).reshape(row_count, head_count, 64), 1e-06) * gain_row
        + offset
    )
    paired = normed.reshape(row_count, head_count, 32, 2)
    first_half = paired[..., 0]
    second = paired[..., 1]
    cosine = jnp.cos(angles)[:, None, :]
    sine_part = jnp.sin(angles)[:, None, :]
    rotated = jnp.stack(
        [first_half * cosine - second * sine_part, first_half * sine_part + second * cosine],
        axis=-1,
    ).reshape(row_count, head_count, 64)
    return jnp.where(is_video[:, None, None], rotated, normed).astype(jnp.bfloat16)


def on_device(
    hidden,
    queries,
    key_proj,
    value_proj,
    norm_gain,
    norm_bias,
    positions,
    text_len,
    time_embed,
    gate_table,
    mod_table,
    out_weight,
    proj_weight,
    proj_bias,
    latent,
    solver_coef,
    step_index,
):
    seq_count = lax.axis_size("seq")
    seq_place = lax.axis_index("seq")
    local_rows = queries.shape[1]
    head_count = queries.shape[2] // 64
    head_group = max(head_count // seq_count, 1)
    row_split = max(seq_count // head_count, 1)
    part_rows = local_rows // row_split
    head_sets = head_count // head_group
    row_index = seq_place * local_rows + jnp.arange(local_rows)
    is_video = row_index >= TEXT_SLOTS
    angles = rotary_angles(positions)
    rot_query = norm_rotate(queries[0], norm_gain[0], norm_bias[0], angles, is_video)
    rot_key = norm_rotate(key_proj[0], norm_gain[1], norm_bias[1], angles, is_video)
    query_send = rot_query.reshape(row_split, part_rows, head_sets, head_group, 64)
    query_send = query_send.transpose(2, 0, 1, 3, 4).reshape(seq_count, part_rows * head_group * 64)

    def spread(values):
        grouped = values.transpose(1, 0, 2)
        widened = jnp.broadcast_to(
            grouped[:, None], (head_sets, row_split, local_rows, head_group * 64)
        )
        return widened.reshape(seq_count, local_rows * head_group * 64)

    key_send = spread(rot_key)
    value_send = spread(value_proj[0].reshape(local_rows, head_count, 64))
    query_recv, key_recv, value_recv = (
        lax.all_to_all(query_send, "seq", split_axis=0, concat_axis=0, tiled=True),
        lax.all_to_all(key_send, "seq", split_axis=0, concat_axis=0, tiled=True),
        lax.all_to_all(value_send, "seq", split_axis=0, concat_axis=0, tiled=True),
    )
    total_keys = seq_count * local_rows
    query_count = seq_count * part_rows
    query_all = query_recv.reshape(query_count, head_group, 64)
    key_index = jnp.arange(total_keys)
    key_valid = (key_index >= TEXT_SLOTS) | (key_index < text_len[0])
    block_keys = math.gcd(512, total_keys)
    block_count = total_keys // block_keys

    def key_step(state_pair, operands):
        numerator, denominator = state_pair
        key_block, value_block, valid_block = operands
        scores = (
            jnp.einsum("qgd,kgd->gqk", query_all, key_block, preferred_element_type=jnp.float32)
            * 0.125
        )
        weights = jnp.where(valid_block[None, None, :], jnp.exp(scores), 0.0)
        denominator = denominator + jnp.sum(weights, axis=2)
        numerator = numerator + jnp.einsum(
            "gqk,kgd->gqd",
            weights.astype(jnp.bfloat16),
            value_block,
            preferred_element_type=jnp.float32,
        )
        return ((numerator, denominator), None)

    start_state = (
        jnp.zeros((head_group, query_count, 64), jnp.float32),
        jnp.zeros((head_group, query_count), jnp.float32),
    )
    scanned = (
        key_recv.reshape(block_count, block_keys, head_group, 64),
        value_recv.reshape(block_count, block_keys, head_group, 64),
        key_valid.reshape(block_count, block_keys),
    )
    final_state, unused_out = lax.scan(key_step, start_state, scanned)
    attended = (final_state[0] / final_state[1][..., None]).astype(jnp.bfloat16)
    back_send = attended.reshape(head_group, seq_count, part_rows, 64).transpose(1, 2, 0, 3)
    back_send = back_send.reshape(seq_count, part_rows * head_group * 64)
    back_recv = lax.all_to_all(back_send, "seq", split_axis=0, concat_axis=0, tiled=True)
    attended_rows = back_recv.reshape(head_sets, row_split, part_rows, head_group, 64)
    attended_rows = attended_rows.transpose(1, 2, 0, 3, 4).reshape(local_rows, head_count * 64)
    embed_act = jax.nn.silu(time_embed.astype(jnp.float32)).astype(jnp.bfloat16)[None, :]
    gate_full, mod_full = (
        lax.all_gather(gate_table, "seq", axis=1, tiled=True),
        lax.all_gather(mod_table, "seq", axis=1, tiled=True),
    )
    gate_vec = jnp.dot(embed_act, gate_full, preferred_element_type=jnp.float32)[0]
    modulation = jnp.dot(embed_act, mod_full, preferred_element_type=jnp.float32)[0]
    projected = jnp.dot(
        attended_rows,
        lax.all_gather(out_weight, ("cfg", "seq"), axis=1, tiled=True),
        preferred_element_type=jnp.float32,
    )
    model_width = hidden.shape[2]
    residual = hidden[0].astype(jnp.float32) + gate_vec[None, :] * projected
    normed = (
        layer_norm(residual, 1e-05) * (1.0 + modulation[model_width:]) + modulation[:model_width]
    )
    normed = normed.astype(jnp.bfloat16)
    prediction = jnp.dot(normed, proj_weight, preferred_element_type=jnp.float32) + proj_bias
    cfg_place = lax.axis_index("cfg")
    own_width = prediction.shape[1] // 2
    own_pred = lax.dynamic_slice_in_dim(prediction, cfg_place * own_width, own_width, 1)
    sent_pred = lax.dynamic_slice_in_dim(prediction, (1 - cfg_place) * own_width, own_width, 1)
    partner = swapped(sent_pred, "cfg", 0)
    is_cond = cfg_place == 0
    cond_pred = jnp.where(is_cond, own_pred, partner)
    uncond_pred = jnp.where(is_cond, partner, own_pred)
    guided = uncond_pred + GUIDANCE * (cond_pred - uncond_pred)
    own_latent = lax.dynamic_slice_in_dim(latent, cfg_place * own_width, own_width, 1)
    step_coefs = lax.dynamic_index_in_dim(solver_coef, step_index[0], axis=1, keepdims=False)
    updated = step_coefs[0] * own_latent + step_coefs[1] * guided
    return jnp.where(is_video[:, None], updated, 0.0)


def solution(mesh):
    placed = (
        P("cfg", "seq", None),
        P("cfg", "seq", None),
        P("cfg", "seq", None),
        P("cfg", "seq", None),
        P(),
        P(),
        P(None, "seq"),
        P("cfg"),
        P(),
        P(None, "seq"),
        P(None, "seq"),
        P(None, ("cfg", "seq")),
        P(),
        P(),
        P("seq", None),
        P(),
        P(),
    )
    return jax.shard_map(
        on_device, mesh=mesh, in_specs=placed, out_specs=P("seq", "cfg"), check_vma=False
    )
```

profile of v0, /device:TPU:1, one launch (start us, length us, event | category | flops | bytes accessed | tf_op | source)
XLA Modules:
  0.0 621.5 jit_solution(9374460455169536504)
XLA Ops:
  8.8 1.2 copy.94
  10.1 0.9 copy.96
  15.2 0.8 multiply_add_fusion
  16.0 0.8 multiply_add_fusion.1
  16.8 3.5 multiply_subtract_fusion
  20.3 1.4 pad_maximum_fusion.1
  21.7 2.1 copy.95
  23.8 2.2 reshape.328
  26.1 1.6 copy.98
  27.7 1.3 rsqrt.30
  29.0 1.3 div.39
  30.4 2.8 fusion.14
  33.2 2.0 copy.100
  36.1 1.8 reduce.27
  38.7 15.3 %all-to-all-start.1 = ((bf16[128,2,384]{2,1,0:T(2,128)(2,1)}), bf16[128,2,384]{2,1,0:T(2,128)(2,1)}, u32[]{:S(2)}, u32[]{:S(2)}) async-start(bf16[128,2,384]{2,1,0:T(2,128)(2,1)} %reshape.368), calls=%async_computation.1 | async-start | bytes 393216 | tf_op jit(solution)/shard_map/all_to_all | solution.py:101
  54.0 1.4 pad_maximum_fusion
  56.1 0.8 fusion.13
  57.7 0.9 all_to_all.32
  58.5 5.3 reduce.26
  63.9 1.5 reshape.366
  65.4 0.8 all-to-all-done.1
  66.2 12.1 %all-to-all-start = ((bf16[128,2,1536]{2,1,0:T(2,128)(2,1)}), bf16[128,2,1536]{2,1,0:T(2,128)(2,1)}, u32[]{:S(2)}, u32[]{:S(2)}) async-start(bf16[128,2,1536]{2,1,0:T(2,128)(2,1)} %reshape.366), calls=%async_computation | async-start | bytes 1572864 | tf_op jit(solution)/shard_map/all_to_all | solution.py:102
  79.0 0.9 all_to_all.34
  79.8 5.3 reduce.28
  85.2 1.5 reshape.370
  86.6 15.1 %all-to-all-done = bf16[128,2,1536]{2,1,0:T(2,128)(2,1)} async-done(((bf16[128,2,1536]{2,1,0:T(2,128)(2,1)}), bf16[128,2,1536]{2,1,0:T(2,128)(2,1)}, u32[]{:S(2)}, u32[]{:S(2)}) %all-to-all-start) | async-done | bytes 786464 | tf_op jit(solution)/shard_map/all_to_all | solution.py:102
  101.8 8.7 %all-to-all-start.2 = ((bf16[128,2,1536]{2,1,0:T(2,128)(2,1)}), bf16[128,2,1536]{2,1,0:T(2,128)(2,1)}, u32[]{:S(2)}, u32[]{:S(2)}) async-start(bf16[128,2,1536]{2,1,0:T(2,128)(2,1)} %reshape.370), calls=%async_computation.2 | async-start | bytes 1572864 | tf_op jit(solution)/shard_map/all_to_all | solution.py:103
  111.2 1.6 reshape.369
  112.7 1.2 reduce.9
  114.3 5.0 reshape.367
  119.3 4.7 reduce.6
  124.1 1.0 reshape.317
  125.1 1.4 copy.104
  126.5 7.3 %all-to-all-done.2 = bf16[128,2,1536]{2,1,0:T(2,128)(2,1)} async-done(((bf16[128,2,1536]{2,1,0:T(2,128)(2,1)}), bf16[128,2,1536]{2,1,0:T(2,128)(2,1)}, u32[]{:S(2)}, u32[]{:S(2)}) %all-to-all-start.2) | async-done | bytes 786464 | tf_op jit(solution)/shard_map/all_to_all | solution.py:103
  133.8 5.3 reshape.371
  139.1 4.7 reduce.10
  143.8 1.0 reshape.320
  145.5 25.9 %while.13 = (s32[]{:T(128)}, f32[1,1536,64]{1,2,0:T(8,128)S(1)}, f32[1,1536]{1,0:T(1,128)S(1)}, pred[12,512]{1,0:T(8,128)(4,1)S(1)}, bf16[12,512,1,64]{1,3,2,0:T...) while((s32[]{:T(128)}, f32[1,1536,64]{1,2,0:T(8,128)S(1)}, ...), condition=%wide.region_6.7_spmd.clone, body=%wide.region_4.6_spmd.clone.sunk | while | flops 204670464 | bytes 4286076 | solution.py:139
  145.6 1.6 fusion.47
  147.7 1.7 fusion.47
  149.9 1.7 fusion.47
  152.0 1.6 fusion.47
  154.2 1.6 fusion.47
  156.4 1.6 fusion.47
  158.5 1.6 fusion.47
  160.7 1.6 fusion.47
  162.9 1.6 fusion.47
  165.0 1.6 fusion.47
  167.2 1.6 fusion.47
  169.3 1.6 fusion.47
  172.0 1.8 reduce.29
  174.5 8.3 %all-to-all-start.3 = ((bf16[128,2,384]{2,1,0:T(2,128)(2,1)}), bf16[128,2,384]{2,1,0:T(2,128)(2,1)S(1)}, u32[]{:S(2)}, u32[]{:S(2)}) async-start(bf16[128,2,384]{2,1,0:T(2,128)(2,1)} %reshape.372), calls=%async_computation.3 | async-start | bytes 393216 | tf_op jit(solution)/shard_map/all_to_all | solution.py:143
  183.6 11.7 %all-to-all-done.3 = bf16[128,2,384]{2,1,0:T(2,128)(2,1)S(1)} async-done(((bf16[128,2,384]{2,1,0:T(2,128)(2,1)}), bf16[128,2,384]{2,1,0:T(2,128)(2,1)S(1)}, u32[]{:S(2)}, u32[]{:S(2)}) %all-to-all-start.3) | async-done | bytes 196640 | tf_op jit(solution)/shard_map/all_to_all | solution.py:143
  195.4 1.2 reduce.12
  197.6 33.6 %all-gather.5.cloned.1.call-done = bf16[512,3072]{0,1:T(8,128)(2,1)} async-done(((bf16[512,24]{0,1:T(8,128)(2,1)}), bf16[512,3072]{0,1:T(8,128)(2,1)}) %all-gather.5.cloned.1.call-update) | async-done | bytes 3145744 | tf_op jit(solution)/shard_map/all_gather | solution.py:148
  231.2 2.8 fusion.30
  234.0 215.7 %all-gather.7.cloned.1.call-done = bf16[512,6144]{0,1:T(8,128)(2,1)} async-done(((bf16[512,48]{0,1:T(8,128)(2,1)}), bf16[512,6144]{0,1:T(8,128)(2,1)}) %all-gather.7.cloned.1.call-update) | async-done | bytes 6291472 | tf_op jit(solution)/shard_map/all_gather | solution.py:149
  449.7 4.5 fusion.31
  454.2 124.8 %all-gather.9.cloned.1.call-done = bf16[256,12,2048]{2,1,0:T(8,128)(2,1)} async-done(((bf16[1,12,2048]{2,1,0:T(8,128)(2,1)}), bf16[256,12,2048]{2,1,0:T(8,128)(2,1)}) %all-gather.9.cloned.1.call-update) | async-done | bytes 12582928 | tf_op jit(solution)/shard_map/all_gather | solution.py:155
  579.0 19.9 %reshape.330 = bf16[3072,2048]{1,0:T(8,128)(2,1)} reshape(bf16[256,12,2048]{2,1,0:T(8,128)(2,1)} %all-gather.9.cloned.1.call-done) | data formatting | bytes 25165824
  598.9 8.6 %fusion.29 = (f32[48]{0:T(128)S(1)}, f32[48,3072]{1,0:T(8,128)S(1)}) fusion(bf16[48,2048]{1,0:T(8,128)(2,1)S(1)} %reshape.322, bf16[3072,2048]{1,0:T(8,128)(2,1)} %reshape.330, f32[3072]{0:T(1024)S(1)} %bitcast.102, bf16[1,48,3072]{2,1,0:T(8,128)(2,1)S(1)} %copy-done.2), kind=kOutput, calls=%fused_computation.81 | convolution fusion | flops 604569536 | bytes 13676736 | tf_op jit(solution)/shard_map/dot_general | solution.py:153
  608.2 2.8 collective-permute-start
  611.6 0.9 collective-permute-done
  612.4 1.4 add_select_fusion
  (142 shorter events, 21.2 us)
Async XLA Ops:
  6.5 601.2 %copy-start = (bf16[3072,64]{0,1:T(8,128)(2,1)S(1)}, bf16[3072,64]{0,1:T(8,128)(2,1)}, u32[]{:S(2)}) copy-start(bf16[3072,64]{0,1:T(8,128)(2,1)} %param.33) | copy-start | bytes 1179652
  6.5 224.7 %all-gather.5.cloned.1.call-start = ((), (), s32[]{:S(2)}) async-start(), calls=%async_computation.4 | async-start | bytes 3170304 | tf_op jit(solution)/shard_map/all_gather | solution.py:148
  7.3 442.4 %all-gather.7.cloned.1.call-start = ((), (), s32[]{:S(2)}) async-start(), calls=%async_computation.5 | async-start | bytes 6340608 | tf_op jit(solution)/shard_map/all_gather | solution.py:149
  8.0 571.0 %all-gather.9.cloned.1.call-start = ((), (), s32[]{:S(2)}) async-start(), calls=%async_computation.6 | async-start | bytes 16842752 | tf_op jit(solution)/shard_map/all_gather | solution.py:155
  8.7 2.3 copy-start.15
  8.8 2.3 copy-start.16
  8.8 3.1 copy-start.12
  8.8 3.1 copy-start.3
  12.5 1.8 copy-start.19
  12.5 1.9 copy-start.18
  15.2 1.6 copy-start.5
  33.2 20.9 %copy-start.1 = (bf16[48,32,32,1]{0,3,2,1:T(2,128)(2,1)S(1)}, bf16[48,32,32,1]{0,3,2,1:T(2,128)(2,1)}, u32[]{:S(2)}) copy-start(bf16[48,32,32,1]{0,3,2,1:T(2,128)(2,1)} %get-tuple-element.122) | copy-start | bytes 294916
  38.7 17.4 %copy-start.6 = (f32[48,32]{0,1:T(8,128)S(1)}, f32[48,32]{0,1:T(8,128)}, u32[]{:S(2)}) copy-start(f32[48,32]{0,1:T(8,128)} %copy-done.5) | copy-start | bytes 18436
  38.7 17.4 %copy-start.10 = (f32[64]{0:T(128)S(1)}, f32[64]{0:T(128)}, u32[]{:S(2)}) copy-start(f32[64]{0:T(128)} %get-tuple-element.135) | copy-start | bytes 772
  38.7 17.4 %copy-start.11 = (f32[64]{0:T(128)S(1)}, f32[64]{0:T(128)}, u32[]{:S(2)}) copy-start(f32[64]{0:T(128)} %get-tuple-element.140) | copy-start | bytes 772
  38.7 27.5 %all-to-all-start.1 = ((bf16[128,2,384]{2,1,0:T(2,128)(2,1)}), bf16[128,2,384]{2,1,0:T(2,128)(2,1)}, u32[]{:S(2)}, u32[]{:S(2)}) async-start(bf16[128,2,384]{2,1,0:T(2,128)(2,1)} %reshape.368), calls=%async_computation.1 | async-start | bytes 393216 | tf_op jit(solution)/shard_map/all_to_all | solution.py:101
  56.0 0.8 copy-start.8
  63.9 14.3 %copy-start.4 = (bf16[1,48,2048]{2,1,0:T(8,128)(2,1)S(1)}, bf16[1,48,2048]{2,1,0:T(8,128)(2,1)}, u32[]{:S(2)}) copy-start(bf16[1,48,2048]{2,1,0:T(8,128)(2,1)} %param.24) | copy-start | bytes 589828
  66.2 35.6 %all-to-all-start = ((bf16[128,2,1536]{2,1,0:T(2,128)(2,1)}), bf16[128,2,1536]{2,1,0:T(2,128)(2,1)}, u32[]{:S(2)}, u32[]{:S(2)}) async-start(bf16[128,2,1536]{2,1,0:T(2,128)(2,1)} %reshape.366), calls=%async_computation | async-start | bytes 1572864 | tf_op jit(solution)/shard_map/all_to_all | solution.py:102
  101.8 32.1 %all-to-all-start.2 = ((bf16[128,2,1536]{2,1,0:T(2,128)(2,1)}), bf16[128,2,1536]{2,1,0:T(2,128)(2,1)}, u32[]{:S(2)}, u32[]{:S(2)}) async-start(bf16[128,2,1536]{2,1,0:T(2,128)(2,1)} %reshape.370), calls=%async_computation.2 | async-start | bytes 1572864 | tf_op jit(solution)/shard_map/all_to_all | solution.py:103
  171.5 11.3 %copy-start.13 = (bf16[512]{0:T(512)(128)(2,1)S(1)}, bf16[512]{0:T(512)(128)(2,1)}, u32[]{:S(2)}) copy-start(bf16[512]{0:T(512)(128)(2,1)} %param.29) | copy-start | bytes 3076
  171.5 12.0 %copy-start.14 = (f32[2,50]{1,0:T(2,128)S(1)}, f32[2,50]{1,0:T(2,128)}, u32[]{:S(2)}) copy-start(f32[2,50]{1,0:T(2,128)} %param.36) | copy-start | bytes 1204
  174.5 20.8 %all-to-all-start.3 = ((bf16[128,2,384]{2,1,0:T(2,128)(2,1)}), bf16[128,2,384]{2,1,0:T(2,128)(2,1)S(1)}, u32[]{:S(2)}, u32[]{:S(2)}) async-start(bf16[128,2,384]{2,1,0:T(2,128)(2,1)} %reshape.372), calls=%async_computation.3 | async-start | bytes 393216 | tf_op jit(solution)/shard_map/all_to_all | solution.py:143
  454.2 144.8 %copy-start.2 = (bf16[1,48,3072]{2,1,0:T(8,128)(2,1)S(1)}, bf16[1,48,3072]{2,1,0:T(8,128)(2,1)}, u32[]{:S(2)}) copy-start(bf16[1,48,3072]{2,1,0:T(8,128)(2,1)} %param.21) | copy-start | bytes 884740
  598.9 8.9 %copy-start.17 = (f32[64]{0:T(128)S(1)}, f32[64]{0:T(128)}, u32[]{:S(2)}) copy-start(f32[64]{0:T(128)} %param.34) | copy-start | bytes 772
  607.5 4.9 copy-start.7
  607.5 4.9 copy-start.9
  608.2 4.2 collective-permute-start
Sparse Core Ops, SparseCore 0:
  9.2 221.9 all-gather.4
  233.1 216.5 all-gather.6
  453.4 125.5 all-gather.8
where the time goes:
time: 632 us; the launch traced here: 622 us
  waiting for transfers between devices  412 us (65%)
  local copies, waits for them, and re-layouts  64.4 us (10%)
  starting transfers between devices  47.2 us (7%)
  matrix products  41.1 us (7%)
  other arithmetic  40.8 us (6%)
  between operations  15.6 us (2%)
    all_gather x1, waiting for transfers between devices, on_device(): lax.all_gather(mod_table, 'seq', axis=1, tiled=True)  216 us
    all_gather x1, waiting for transfers between devices, on_device(): lax.all_gather(out_weight, ('cfg', 'seq'), axis=1, tiled=True)  125 us
    unnamed x54, local copies, waits for them, and re-layouts  40.2 us
    all_gather x1, waiting for transfers between devices, on_device(): lax.all_gather(gate_table, 'seq', axis=1, tiled=True)  33.6 us
    dot_general x12, matrix products, key_step(): jnp.einsum('qgd,kgd->gqk', query_all, key_block, preferred_element_type=j...  19.8 us
    all_to_all x1, starting transfers between devices, on_device(): lax.all_to_all(query_send, 'seq', split_axis=0, concat_axis=0, tiled=True)  15.3 us
    all_to_all x1, waiting for transfers between devices, on_device(): lax.all_to_all(key_send, 'seq', split_axis=0, concat_axis=0, tiled=True)  15.1 us
  transfers between devices with their start and end apart: 8, of which 8 were waited for; matrix products, arithmetic and copies ran while one was open for 18% of the time, Pallas kernels for 0%

commit v1 on v0

--- a/solution.py
+++ b/solution.py
@@ -152,7 +152,12 @@
     modulation = jnp.dot(embed_act, mod_full, preferred_element_type=jnp.float32)[0]
     projected = jnp.dot(
         attended_rows,
-        lax.all_gather(out_weight, ("cfg", "seq"), axis=1, tiled=True),
+        jnp.concatenate(
+            lax.all_to_all(
+                jnp.stack([out_weight] * lax.axis_size(("cfg", "seq"))), ("cfg", "seq"), 0, 0
+            ),
+            axis=1,
+        ),
         preferred_element_type=jnp.float32,
     )
     model_width = hidden.shape[2]

time: 632 us -> 795 us (1.26)
  waiting for transfers between devices: 412 us -> 547 us
  blocking collectives: 0 us -> 19.4 us
    all_gather x1, waiting for transfers between devices: 33.6 us -> 264 us  [on_device(): lax.all_gather(gate_table, 'seq', axis=1, tiled=True)]
    all_gather x1 -> x0, waiting for transfers between devices: 125 us -> none  [on_device(): lax.all_gather(out_weight, ('cfg', 'seq'), axis=1, tiled=True)]
    all_gather x1, waiting for transfers between devices: 216 us -> 258 us  [on_device(): lax.all_gather(mod_table, 'seq', axis=1, tiled=True)]
    unnamed x54 -> x55, local copies, waits for them, and re-layouts: 40.2 us -> 19.6 us
    reshape x0 -> x1, local copies, waits for them, and re-layouts: none -> 20 us  [on_device(): jnp.concatenate(lax.all_to_all(jnp.stack([out_weight] * lax.axis_size(('c...]
    all_to_all x0 -> x1, blocking collectives: none -> 19.4 us  [on_device(): lax.all_to_all(back_send, 'seq', split_axis=0, concat_axis=0, tiled=True)]
    all_to_all x1, waiting for transfers between devices: 11.7 us -> 0.01 us  [on_device(): lax.all_to_all(jnp.stack([out_weight] * lax.axis_size(('cfg', 'seq'))), (...]
  transfers between devices with their start and end apart: 8 -> 7, of which waited for: 8 -> 6; matrix products, arithmetic and copies ran while one was open for 18% -> 6% of each run, Pallas kernels for 0% -> 0%
where the time goes in v1:
time: 795 us; the launch traced here: 783 us
  waiting for transfers between devices  547 us (69%)
  local copies, waits for them, and re-layouts  69.7 us (9%)
  starting transfers between devices  48.5 us (6%)
  matrix products  41.1 us (5%)
  other arithmetic  40.5 us (5%)
  blocking collectives  19.4 us (2%)
  between operations  15.9 us (2%)
    all_gather x1, waiting for transfers between devices, on_device(): lax.all_gather(gate_table, 'seq', axis=1, tiled=True)  264 us
    all_gather x1, waiting for transfers between devices, on_device(): lax.all_gather(mod_table, 'seq', axis=1, tiled=True)  258 us
    reshape x1, local copies, waits for them, and re-layouts, on_device(): jnp.concatenate(lax.all_to_all(jnp.stack([out_weight] * lax.axis_size(('c...  20 us
    dot_general x12, matrix products, key_step(): jnp.einsum('qgd,kgd->gqk', query_all, key_block, preferred_element_type=j...  19.8 us
    unnamed x55, local copies, waits for them, and re-layouts  19.6 us
    all_to_all x1, blocking collectives, on_device(): lax.all_to_all(back_send, 'seq', split_axis=0, concat_axis=0, tiled=True)  19.4 us
  transfers between devices with their start and end apart: 7, of which 6 were waited for; matrix products, arithmetic and copies ran while one was open for 6% of the time, Pallas kernels for 0%

profile of v1, /device:TPU:1, one launch (start us, length us, event | category | flops | bytes accessed | tf_op | source)
XLA Modules:
  0.0 782.6 jit_solution(6987173073581660519)
XLA Ops:
  6.5 1.2 copy.95
  7.9 1.0 copy.97
  12.9 0.8 multiply_add_fusion
  13.9 0.8 multiply_add_fusion.1
  14.7 3.5 multiply_subtract_fusion
  18.2 1.4 pad_maximum_fusion.1
  19.5 2.1 copy.96
  21.7 2.2 reshape.338
  23.9 1.6 copy.99
  25.5 1.3 rsqrt.30
  26.9 1.3 div.39
  28.2 2.8 fusion.14
  31.0 2.0 copy.101
  33.9 1.7 reduce.27
  35.6 0.7 reshape.376
  36.4 15.3 %all-to-all-start.1 = ((bf16[128,2,384]{2,1,0:T(2,128)(2,1)}), bf16[128,2,384]{2,1,0:T(2,128)(2,1)}, u32[]{:S(2)}, u32[]{:S(2)}) async-start(bf16[128,2,384]{2,1,0:T(2,128)(2,1)} %reshape.376), calls=%async_computation.1 | async-start | bytes 393216 | tf_op jit(solution)/shard_map/all_to_all | solution.py:101
  51.7 1.4 pad_maximum_fusion
  53.7 0.8 fusion.13
  55.3 0.9 all_to_all.36
  56.2 5.3 reduce.26
  61.5 1.5 reshape.374
  63.0 0.9 all-to-all-done.1
  63.8 12.6 %all-to-all-start = ((bf16[128,2,1536]{2,1,0:T(2,128)(2,1)}), bf16[128,2,1536]{2,1,0:T(2,128)(2,1)}, u32[]{:S(2)}, u32[]{:S(2)}) async-start(bf16[128,2,1536]{2,1,0:T(2,128)(2,1)} %reshape.374), calls=%async_computation | async-start | bytes 1572864 | tf_op jit(solution)/shard_map/all_to_all | solution.py:102
  77.2 0.9 all_to_all.38
  78.0 5.3 reduce.28
  83.3 1.4 reshape.378
  84.8 15.0 %all-to-all-done = bf16[128,2,1536]{2,1,0:T(2,128)(2,1)} async-done(((bf16[128,2,1536]{2,1,0:T(2,128)(2,1)}), bf16[128,2,1536]{2,1,0:T(2,128)(2,1)}, u32[]{:S(2)}, u32[]{:S(2)}) %all-to-all-start) | async-done | bytes 786464 | tf_op jit(solution)/shard_map/all_to_all | solution.py:102
  99.8 7.8 all-to-all-start.2
  108.2 1.6 reshape.377
  109.8 1.2 reduce.9
  111.4 5.0 reshape.375
  116.4 4.7 reduce.6
  121.2 1.0 reshape.325
  122.2 1.4 copy.105
  123.6 7.3 all-to-all-done.2
  130.9 5.3 reshape.379
  136.2 4.7 reduce.10
  140.9 1.0 reshape.328
  142.6 25.9 %while.13 = (s32[]{:T(128)}, f32[1,1536,64]{1,2,0:T(8,128)S(1)}, f32[1,1536]{1,0:T(1,128)S(1)}, pred[12,512]{1,0:T(8,128)(4,1)S(1)}, bf16[12,512,1,64]{1,3,2,0:T...) while((s32[]{:T(128)}, f32[1,1536,64]{1,2,0:T(8,128)S(1)}, ...), condition=%wide.region_6.7_spmd.clone, body=%wide.region_4.6_spmd.clone.sunk | while | flops 204670464 | bytes 4286076 | solution.py:139
  142.6 1.6 fusion.47
  144.8 1.6 fusion.47
  147.0 1.6 fusion.47
  149.1 1.6 fusion.47
  151.3 1.6 fusion.47
  153.5 1.6 fusion.47
  155.6 1.6 fusion.47
  157.8 1.6 fusion.47
  159.9 1.6 fusion.47
  162.1 1.6 fusion.47
  164.3 1.6 fusion.47
  166.4 1.6 fusion.47
  169.1 1.7 reduce.29
  170.9 19.4 %all_to_all.45 = bf16[128,2,384]{2,1,0:T(2,128)(2,1)S(1)} all-to-all(bf16[128,2,384]{2,1,0:T(2,128)(2,1)S(1)} %reshape.380), channel_id=1, replica_groups=mesh['cfg'=2,'seq'=128] {'seq'}, dimensions={0} | all-to-all | bytes 393216 | tf_op jit(solution)/shard_map/all_to_all | solution.py:143
  190.3 5.9 stack.8
  196.2 8.3 %all-to-all-start.4 = ((bf16[256,2048,12]{1,2,0:T(8,128)(2,1)}), bf16[256,2048,12]{1,2,0:T(8,128)(2,1)}, u32[]{:S(2)}, u32[]{:S(2)}) async-start(bf16[256,2048,12]{1,2,0:T(8,128)(2,1)} %stack.8), calls=%async_computation.4 | async-start | bytes 33554432 | tf_op jit(solution)/shard_map/all_to_all | solution.py:156
  206.9 1.2 reduce.12
  209.0 264.3 %all-gather.3.cloned.1.call-done = bf16[512,3072]{0,1:T(8,128)(2,1)} async-done(((bf16[512,24]{0,1:T(8,128)(2,1)}), bf16[512,3072]{0,1:T(8,128)(2,1)}) %all-gather.3.cloned.1.call-update) | async-done | bytes 3145744 | tf_op jit(solution)/shard_map/all_gather | solution.py:148
  473.4 2.8 fusion.30
  476.2 257.8 %all-gather.5.cloned.1.call-done = bf16[512,6144]{0,1:T(8,128)(2,1)} async-done(((bf16[512,48]{0,1:T(8,128)(2,1)}), bf16[512,6144]{0,1:T(8,128)(2,1)}) %all-gather.5.cloned.1.call-update) | async-done | bytes 6291472 | tf_op jit(solution)/shard_map/all_gather | solution.py:149
  733.9 4.5 fusion.31
  738.5 20.0 %reshape.332 = bf16[2048,3072]{0,1:T(8,128)(2,1)} reshape(bf16[2048,256,12]{0,2,1:T(8,128)(2,1)} %bitcast.23) | data formatting | bytes 25165824 | tf_op jit(solution)/shard_map/reshape | solution.py:155
  758.4 8.6 %fusion.29 = (f32[48]{0:T(128)S(1)}, f32[48,3072]{1,0:T(8,128)S(1)}) fusion(bf16[48,2048]{1,0:T(8,128)(2,1)S(1)} %reshape.330, bf16[2048,3072]{0,1:T(8,128)(2,1)} %reshape.332, f32[3072]{0:T(1024)S(1)} %bitcast.101, bf16[1,48,3072]{2,1,0:T(8,128)(2,1)S(1)} %copy-done.2), kind=kOutput, calls=%fused_computation.81 | convolution fusion | flops 604569536 | bytes 13676736 | tf_op jit(solution)/shard_map/dot_general | solution.py:153
  767.7 4.3 collective-permute-start
  773.2 1.4 add_select_fusion
  (143 shorter events, 19.7 us)
Async XLA Ops:
  6.5 760.8 %copy-start = (bf16[3072,64]{0,1:T(8,128)(2,1)S(1)}, bf16[3072,64]{0,1:T(8,128)(2,1)}, u32[]{:S(2)}) copy-start(bf16[3072,64]{0,1:T(8,128)(2,1)} %param.33) | copy-start | bytes 1179652
  7.9 2.0 copy-start.16
  7.9 2.0 copy-start.17
  7.9 2.8 copy-start.13
  7.9 2.8 copy-start.3
  11.0 1.8 copy-start.20
  11.4 2.2 copy-start.19
  12.1 2.6 copy-start.5
  31.0 20.7 %copy-start.1 = (bf16[48,32,32,1]{0,3,2,1:T(2,128)(2,1)S(1)}, bf16[48,32,32,1]{0,3,2,1:T(2,128)(2,1)}, u32[]{:S(2)}) copy-start(bf16[48,32,32,1]{0,3,2,1:T(2,128)(2,1)} %get-tuple-element.122) | copy-start | bytes 294916
  36.4 17.4 %copy-start.6 = (f32[48,32]{0,1:T(8,128)S(1)}, f32[48,32]{0,1:T(8,128)}, u32[]{:S(2)}) copy-start(f32[48,32]{0,1:T(8,128)} %copy-done.5) | copy-start | bytes 18436
  36.4 17.4 %copy-start.11 = (f32[64]{0:T(128)S(1)}, f32[64]{0:T(128)}, u32[]{:S(2)}) copy-start(f32[64]{0:T(128)} %get-tuple-element.135) | copy-start | bytes 772
  36.4 17.4 %copy-start.12 = (f32[64]{0:T(128)S(1)}, f32[64]{0:T(128)}, u32[]{:S(2)}) copy-start(f32[64]{0:T(128)} %get-tuple-element.140) | copy-start | bytes 772
  36.4 27.5 %all-to-all-start.1 = ((bf16[128,2,384]{2,1,0:T(2,128)(2,1)}), bf16[128,2,384]{2,1,0:T(2,128)(2,1)}, u32[]{:S(2)}, u32[]{:S(2)}) async-start(bf16[128,2,384]{2,1,0:T(2,128)(2,1)} %reshape.376), calls=%async_computation.1 | async-start | bytes 393216 | tf_op jit(solution)/shard_map/all_to_all | solution.py:101
  53.7 0.8 copy-start.9
  61.5 14.9 %copy-start.4 = (bf16[1,48,2048]{2,1,0:T(8,128)(2,1)S(1)}, bf16[1,48,2048]{2,1,0:T(8,128)(2,1)}, u32[]{:S(2)}) copy-start(bf16[1,48,2048]{2,1,0:T(8,128)(2,1)} %param.24) | copy-start | bytes 589828
  63.8 35.9 %all-to-all-start = ((bf16[128,2,1536]{2,1,0:T(2,128)(2,1)}), bf16[128,2,1536]{2,1,0:T(2,128)(2,1)}, u32[]{:S(2)}, u32[]{:S(2)}) async-start(bf16[128,2,1536]{2,1,0:T(2,128)(2,1)} %reshape.374), calls=%async_computation | async-start | bytes 1572864 | tf_op jit(solution)/shard_map/all_to_all | solution.py:102
  99.8 31.2 %all-to-all-start.2 = ((bf16[128,2,1536]{2,1,0:T(2,128)(2,1)}), bf16[128,2,1536]{2,1,0:T(2,128)(2,1)}, u32[]{:S(2)}, u32[]{:S(2)}) async-start(bf16[128,2,1536]{2,1,0:T(2,128)(2,1)} %reshape.378), calls=%async_computation.2 | async-start | bytes 1572864 | tf_op jit(solution)/shard_map/all_to_all | solution.py:103
  168.6 21.7 %copy-start.7 = (bf16[2048,12]{0,1:T(8,128)(2,1)S(1)}, bf16[2048,12]{0,1:T(8,128)(2,1)}, u32[]{:S(2)}) copy-start(bf16[2048,12]{0,1:T(8,128)(2,1)} %param.32) | copy-start | bytes 147460
  196.2 9.8 %copy-start.14 = (bf16[512]{0:T(512)(128)(2,1)S(1)}, bf16[512]{0:T(512)(128)(2,1)}, u32[]{:S(2)}) copy-start(bf16[512]{0:T(512)(128)(2,1)} %param.29) | copy-start | bytes 3076
  196.2 10.4 %copy-start.15 = (f32[2,50]{1,0:T(2,128)S(1)}, f32[2,50]{1,0:T(2,128)}, u32[]{:S(2)}) copy-start(f32[2,50]{1,0:T(2,128)} %param.36) | copy-start | bytes 1204
  196.2 542.2 %all-to-all-start.4 = ((bf16[256,2048,12]{1,2,0:T(8,128)(2,1)}), bf16[256,2048,12]{1,2,0:T(8,128)(2,1)}, u32[]{:S(2)}, u32[]{:S(2)}) async-start(bf16[256,2048,12]{1,2,0:T(8,128)(2,1)} %stack.8), calls=%async_computation.4 | async-start | bytes 33554432 | tf_op jit(solution)/shard_map/all_to_all | solution.py:156
  204.5 268.9 %all-gather.3.cloned.1.call-start = ((), (), s32[]{:S(2)}) async-start(), calls=%async_computation.5 | async-start | bytes 3170304 | tf_op jit(solution)/shard_map/all_gather | solution.py:148
  205.2 528.7 %all-gather.5.cloned.1.call-start = ((), (), s32[]{:S(2)}) async-start(), calls=%async_computation.6 | async-start | bytes 6340608 | tf_op jit(solution)/shard_map/all_gather | solution.py:149
  738.5 20.0 %copy-start.2 = (bf16[1,48,3072]{2,1,0:T(8,128)(2,1)S(1)}, bf16[1,48,3072]{2,1,0:T(8,128)(2,1)}, u32[]{:S(2)}) copy-start(bf16[1,48,3072]{2,1,0:T(8,128)(2,1)} %param.21) | copy-start | bytes 884740
  758.4 8.9 %copy-start.18 = (f32[64]{0:T(128)S(1)}, f32[64]{0:T(128)}, u32[]{:S(2)}) copy-start(f32[64]{0:T(128)} %param.34) | copy-start | bytes 772
  767.0 6.2 copy-start.8
  767.0 6.2 copy-start.10
  767.7 5.5 collective-permute-start
Sparse Core Ops, SparseCore 0:
  207.2 266.1 all-gather.2
  475.2 258.6 all-gather.4
